TPU v7x, 1024 devices: a whole 4x8x16 slice. The times are simulated.
1024 devices in a mesh: layer: 2 (over x_hi), row: 64 (over z, x_lo, core), col: 8 (over y).
Axes of the slice: x: 4 (x_hi: 2, x_lo: 2; x = x_hi * 2 + x_lo), y: 8, z: 16, core: 2. Of those that a mesh axis runs over, the one named last changes fastest.
Arguments:
- slab_tiles: bfloat16 [128, 256, 2, 8, 128], P(None, 'row', 'layer'), may hold values from -0.0390625 to 0.0390625
- x_tiles: bfloat16 [1024, 8, 2, 128, 128], P(('layer', 'row', 'col')), may hold values from -6 to 6
- x_cols: int32 [1024, 8, 2], P(('layer', 'row', 'col')), may hold values from 0 to 1023, as said below
- x2_tiles: bfloat16 [1024, 8, 2, 128, 128], P(('layer', 'row', 'col')), may hold values from -6 to 6
- x2_cols: int32 [1024, 8, 2], P(('layer', 'row', 'col')), may hold values from 0 to 1023, as said below
- requests: int32 [2, 64, 8], P('layer'), may hold values from 0 to 1023, as said below
- out_cols: int32 [64, 8, 4], P('row', 'col'), may hold values from 0 to 1023, as said below
Outputs:
- purified: bfloat16 [128, 256, 8, 4, 128], P('layer', 'row', 'col')
Inputs may be any that keep to these rules, and one draw needn't show every extreme that they name: Block row k is held by the device at index k of layer, row and col taken together. requests[l, r, q] is a block row held by layer l at row index (r + q * 8) % 64; every block row held by layer l is named exactly once in requests[l]. out_cols[r, c] holds 4 distinct block columns j, each with j % 8 == c. x_cols[k, c] holds 2 distinct block columns taken from out_cols[r, c], where r is the group whose requests name k. x2_cols[k, c] holds 2 distinct block columns taken from out_cols[r, c], where r is the group whose requests name k.
All inputs are finite; a program needn't handle non-finite values.
Results may differ from a plain program's by a relative error of at most 0.001.
Values may be sent and summed in bfloat16 or wider, within the bound.
A program may use at most 32 MiB of HBM per device.

v0:
```python
import jax
import jax.numpy as jnp
from jax import lax
from jax.sharding import PartitionSpec as P


def as_sent(shard):
    return jax.tree.map(lambda a: a.astype(jnp.bfloat16) if a.dtype == jnp.float32 else a, shard)


def shifted(block, axis, distance):
    devices = range(lax.axis_size(axis))
    route = [((i - distance) % len(devices), i) for i in devices]
    return lax.ppermute(block, axis, route)


def choose_tiles(tile_set, col_ids, targets):
    matches = (col_ids[:, :, None] == targets[None, None, :]).astype(jnp.bfloat16)
    chosen = jnp.einsum("qus,qubd->qbsd", matches, tile_set, preferred_element_type=jnp.float32)
    return chosen.astype(jnp.bfloat16).reshape(
        tile_set.shape[0] * tile_set.shape[2], targets.shape[0] * tile_set.shape[3]
    )


def body(slab_tiles, x_tiles, x_cols, x2_tiles, x2_cols, requests, out_cols):
    grid_rows = lax.axis_size("row")
    col_groups = lax.axis_size("col")
    stride = grid_rows // col_groups
    arrived = (
        lax.all_to_all(x_tiles, "col", split_axis=1, concat_axis=0, tiled=True),
        lax.all_to_all(x_cols, "col", split_axis=1, concat_axis=0, tiled=True),
        lax.all_to_all(x2_tiles, "col", split_axis=1, concat_axis=0, tiled=True),
        lax.all_to_all(x2_cols, "col", split_axis=1, concat_axis=0, tiled=True),
    )
    held_first, first_ids, held_second, second_ids = arrived
    own_row = lax.axis_index("row")
    wanted = requests[0]

    def pick_held(values, owner):
        return lax.dynamic_index_in_dim(values, owner, 0, keepdims=False)[0]

    got_first, got_first_ids, got_second, got_second_ids = ([], [], [], [])
    for slot in range(col_groups):
        offset = slot * stride
        reader = (own_row - offset + grid_rows) % grid_rows
        owner = lax.dynamic_index_in_dim(wanted[:, slot], reader, 0, keepdims=False) % col_groups
        sent = (
            pick_held(held_first, owner),
            pick_held(first_ids, owner),
            pick_held(held_second, owner),
            pick_held(second_ids, owner),
        )
        back = shifted(
            (sent[0], as_sent(sent[1]), sent[2], as_sent(sent[3])),
            "row",
            (grid_rows - offset) % grid_rows,
        )
        got_first.append(back[0])
        got_first_ids.append(back[1])
        got_second.append(back[2])
        got_second_ids.append(back[3])
    targets = out_cols[0, 0]
    chosen_first = choose_tiles(jnp.stack(got_first), jnp.stack(got_first_ids), targets)
    chosen_second = choose_tiles(jnp.stack(got_second), jnp.stack(got_second_ids), targets)
    layer_rows = slab_tiles.shape[0] // lax.axis_size("layer")

    def slab_rows(row_count):
        return slab_tiles.reshape(
            row_count * slab_tiles.shape[1], slab_tiles.shape[3] * slab_tiles.shape[4]
        )

    def term_shape(row_count):
        return (row_count, slab_tiles.shape[1], 1, targets.shape[0], slab_tiles.shape[4])

    product = jnp.dot(
        slab_rows(lax.axis_size("layer") * layer_rows),
        chosen_first,
        preferred_element_type=jnp.float32,
    )
    first_sum = lax.psum_scatter(
        product.reshape(term_shape(lax.axis_size("layer") * layer_rows)),
        "layer",
        scatter_dimension=0,
        tiled=True,
    )
    product = jnp.dot(
        slab_rows(lax.axis_size("layer") * layer_rows),
        chosen_second,
        preferred_element_type=jnp.float32,
    )
    second_sum = lax.psum_scatter(
        product.reshape(term_shape(lax.axis_size("layer") * layer_rows)),
        "layer",
        scatter_dimension=0,
        tiled=True,
    )
    summed = 4.0 * first_sum - 3.0 * second_sum
    return summed.astype(jnp.bfloat16)


def solution(mesh):
    placed = (
        P(None, "row", "layer", None, None),
        P(("layer", "row", "col"), None, None, None, None),
        P(("layer", "row", "col"), None, None),
        P(("layer", "row", "col"), None, None, None, None),
        P(("layer", "row", "col"), None, None),
        P("layer", None, None),
        P("row", "col", None),
    )
    return jax.shard_map(
        body,
        mesh=mesh,
        in_specs=placed,
        out_specs=P("layer", "row", "col", None, None),
        check_vma=False,
    )
```

profile of v0, /device:TPU:6, one launch (start us, length us, event | category | flops | bytes accessed | tf_op | source)
XLA Modules:
  0.0 304.7 jit_solution(11002396705347224142)
XLA Ops:
  6.5 1.3 copy.118
  7.9 7.1 %all-to-all-start.1 = ((s32[1,8,2]{2,0,1:T(1,128)}), s32[1,8,2]{2,0,1:T(1,128)S(1)}, u32[]{:S(2)}, u32[]{:S(2)}) async-start(s32[1,8,2]{2,0,1:T(1,128)} %copy.118), calls=%async_computation.1 | async-start | bytes 8192 | tf_op jit(solution)/shard_map/all_to_all | solution.py:31
  15.7 6.9 %all-to-all-done.1 = s32[1,8,2]{2,0,1:T(1,128)S(1)} async-done(((s32[1,8,2]{2,0,1:T(1,128)}), s32[1,8,2]{2,0,1:T(1,128)S(1)}, u32[]{:S(2)}, u32[]{:S(2)}) %all-to-all-start.1) | async-done | bytes 96 | tf_op jit(solution)/shard_map/all_to_all | solution.py:31
  22.6 10.1 %all_to_all.16 = s32[1,8,2]{2,0,1:T(1,128)S(1)} all-to-all(s32[1,8,2]{2,0,1:T(1,128)S(1)} %copy.130), channel_id=1, replica_groups=mesh['layer'=2,'row'=64,'col'=8] {'col'}, dimensions={1} | all-to-all | bytes 128 | tf_op jit(solution)/shard_map/all_to_all | solution.py:33
  32.7 18.7 %all_to_all.17 = bf16[1,8,2,128,128]{4,3,2,0,1:T(8,128)(2,1)S(1)} all-to-all(bf16[1,8,2,128,128]{4,3,2,0,1:T(8,128)(2,1)} %bitcast.197), channel_id=1, replica_groups=mesh['layer'=2,'row'=64,'col'=8] {'col'}, dimensions={1} | all-to-all | bytes 1048576 | tf_op jit(solution)/shard_map/all_to_all | solution.py:30
  51.4 3.5 %all-to-all-start.2 = ((bf16[1,8,2,128,128]{4,3,2,0,1:T(8,128)(2,1)}), bf16[1,8,2,128,128]{4,3,2,0,1:T(8,128)(2,1)S(1)}, u32[]{:S(2)}, u32[]{:S(2)}) async-start(bf16[1,8,2,128,128]{4,3,2,0,1:T(8,128)(2,1)} %bitcast.47), calls=%async_computation.2 | async-start | bytes 1048576 | tf_op jit(solution)/shard_map/all_to_all | solution.py:32
  73.1 18.2 %collective-permute-start.9 = (s32[2]{0:T(128)S(1)}, s32[2]{0:T(128)S(1)}, u32[]{:S(2)}, u32[]{:S(2)}) collective-permute-start(s32[2]{0:T(128)S(1)} %get-tuple-element.27), channel_id=1, source_target_pairs={{64,0},{72,8},{80,16},{88,24},{96,32},{104,40},{112,48},{120,56},{... | collective-permute-start | bytes 32 | tf_op jit(solution)/shard_map/ppermute | solution.py:14
  91.4 3.6 %collective-permute-start.10 = (s32[2]{0:T(128)S(1)}, s32[2]{0:T(128)S(1)}, u32[]{:S(2)}, u32[]{:S(2)}) collective-permute-start(s32[2]{0:T(128)S(1)} %get-tuple-element.26), channel_id=1, source_target_pairs={{128,0},{136,8},{144,16},{152,24},{160,32},{168,40},{176,48},{184,... | collective-permute-start | bytes 32 | tf_op jit(solution)/shard_map/ppermute | solution.py:14
  95.0 1.9 collective-permute-start.11
  96.9 11.4 %collective-permute-start.12 = (s32[2]{0:T(128)S(1)}, s32[2]{0:T(128)S(1)}, u32[]{:S(2)}, u32[]{:S(2)}) collective-permute-start(s32[2]{0:T(128)S(1)} %get-tuple-element.24), channel_id=1, source_target_pairs={{256,0},{264,8},{272,16},{280,24},{288,32},{296,40},{304,48},{312,... | collective-permute-start | bytes 32 | tf_op jit(solution)/shard_map/ppermute | solution.py:14
  108.4 1.9 collective-permute-start.13
  110.4 5.5 %collective-permute-start.14 = (s32[2]{0:T(128)S(1)}, s32[2]{0:T(128)S(1)}, u32[]{:S(2)}, u32[]{:S(2)}) collective-permute-start(s32[2]{0:T(128)S(1)} %get-tuple-element.22), channel_id=1, source_target_pairs={{384,0},{392,8},{400,16},{408,24},{416,32},{424,40},{432,48},{440,... | collective-permute-start | bytes 32 | tf_op jit(solution)/shard_map/ppermute | solution.py:14
  115.9 6.0 %collective-permute-start.15 = (s32[2]{0:T(128)S(1)}, s32[2]{0:T(128)S(1)}, u32[]{:S(2)}, u32[]{:S(2)}) collective-permute-start(s32[2]{0:T(128)S(1)} %get-tuple-element.21), channel_id=1, source_target_pairs={{448,0},{456,8},{464,16},{472,24},{480,32},{488,40},{496,48},{504,... | collective-permute-start | bytes 32 | tf_op jit(solution)/shard_map/ppermute | solution.py:14
  121.9 1.9 collective-permute-start.25
  123.9 6.1 %collective-permute-start.26 = (s32[2]{0:T(128)S(1)}, s32[2]{0:T(128)S(1)}, u32[]{:S(2)}, u32[]{:S(2)}) collective-permute-start(s32[2]{0:T(128)S(1)} %get-tuple-element.34), channel_id=1, source_target_pairs={{128,0},{136,8},{144,16},{152,24},{160,32},{168,40},{176,48},{184,... | collective-permute-start | bytes 32 | tf_op jit(solution)/shard_map/ppermute | solution.py:14
  130.0 7.8 %collective-permute-start.27 = (s32[2]{0:T(128)S(1)}, s32[2]{0:T(128)S(1)}, u32[]{:S(2)}, u32[]{:S(2)}) collective-permute-start(s32[2]{0:T(128)S(1)} %get-tuple-element.33), channel_id=1, source_target_pairs={{192,0},{200,8},{208,16},{216,24},{224,32},{232,40},{240,48},{248,... | collective-permute-start | bytes 32 | tf_op jit(solution)/shard_map/ppermute | solution.py:14
  137.8 3.7 %collective-permute-start.28 = (s32[2]{0:T(128)S(1)}, s32[2]{0:T(128)S(1)}, u32[]{:S(2)}, u32[]{:S(2)}) collective-permute-start(s32[2]{0:T(128)S(1)} %get-tuple-element.32), channel_id=1, source_target_pairs={{256,0},{264,8},{272,16},{280,24},{288,32},{296,40},{304,48},{312,... | collective-permute-start | bytes 32 | tf_op jit(solution)/shard_map/ppermute | solution.py:14
  141.6 9.0 %collective-permute-start.29 = (s32[2]{0:T(128)S(1)}, s32[2]{0:T(128)S(1)}, u32[]{:S(2)}, u32[]{:S(2)}) collective-permute-start(s32[2]{0:T(128)S(1)} %get-tuple-element.31), channel_id=1, source_target_pairs={{320,0},{328,8},{336,16},{344,24},{352,32},{360,40},{368,48},{376,... | collective-permute-start | bytes 32 | tf_op jit(solution)/shard_map/ppermute | solution.py:14
  150.6 6.1 %collective-permute-start.30 = (s32[2]{0:T(128)S(1)}, s32[2]{0:T(128)S(1)}, u32[]{:S(2)}, u32[]{:S(2)}) collective-permute-start(s32[2]{0:T(128)S(1)} %get-tuple-element.30), channel_id=1, source_target_pairs={{384,0},{392,8},{400,16},{408,24},{416,32},{424,40},{432,48},{440,... | collective-permute-start | bytes 32 | tf_op jit(solution)/shard_map/ppermute | solution.py:14
  156.8 1.9 collective-permute-start.31
  158.7 1.3 collective-permute-done.30
  160.0 4.3 %collective-permute-done.31 = s32[2]{0:T(128)S(1)} collective-permute-done((s32[2]{0:T(128)S(1)}, s32[2]{0:T(128)S(1)}, u32[]{:S(2)}, u32[]{:S(2)}) %collective-permute-start.31) | collective-permute-done | bytes 40 | tf_op jit(solution)/shard_map/ppermute | solution.py:14
  164.6 2.5 collective-permute-start.1
  167.1 3.6 %collective-permute-start.2 = (bf16[2,128,128]{2,0,1:T(2,128)(2,1)S(1)}, bf16[2,128,128]{2,0,1:T(2,128)(2,1)S(1)}, u32[]{:S(2)}, u32[]{:S(2)}) collective-permute-start(bf16[2,128,128]{2,0,1:T(2,128)(2,1)S(1)} %bitcast.211), channel_id=1, source_target_pairs={{128,0},{136,8},{144,16},{152,24},{160,32},{168,40},{176,48},{184,... | collective-permute-start | bytes 196616 | tf_op jit(solution)/shard_map/ppermute | solution.py:14
  170.8 5.6 %collective-permute-start.3 = (bf16[2,128,128]{2,0,1:T(2,128)(2,1)S(1)}, bf16[2,128,128]{2,0,1:T(2,128)(2,1)S(1)}, u32[]{:S(2)}, u32[]{:S(2)}) collective-permute-start(bf16[2,128,128]{2,0,1:T(2,128)(2,1)S(1)} %bitcast.210), channel_id=1, source_target_pairs={{192,0},{200,8},{208,16},{216,24},{224,32},{232,40},{240,48},{248,... | collective-permute-start | bytes 196616 | tf_op jit(solution)/shard_map/ppermute | solution.py:14
  176.5 9.0 %collective-permute-start.4 = (bf16[2,128,128]{2,0,1:T(2,128)(2,1)S(1)}, bf16[2,128,128]{2,0,1:T(2,128)(2,1)S(1)}, u32[]{:S(2)}, u32[]{:S(2)}) collective-permute-start(bf16[2,128,128]{2,0,1:T(2,128)(2,1)S(1)} %bitcast.209), channel_id=1, source_target_pairs={{256,0},{264,8},{272,16},{280,24},{288,32},{296,40},{304,48},{312,... | collective-permute-start | bytes 196616 | tf_op jit(solution)/shard_map/ppermute | solution.py:14
  186.4 4.3 %collective-permute-start.5 = (bf16[2,128,128]{2,0,1:T(2,128)(2,1)S(1)}, bf16[2,128,128]{2,0,1:T(2,128)(2,1)S(1)}, u32[]{:S(2)}, u32[]{:S(2)}) collective-permute-start(bf16[2,128,128]{2,0,1:T(2,128)(2,1)S(1)} %bitcast.208), channel_id=1, source_target_pairs={{320,0},{328,8},{336,16},{344,24},{352,32},{360,40},{368,48},{376,... | collective-permute-start | bytes 196616 | tf_op jit(solution)/shard_map/ppermute | solution.py:14
  190.9 3.7 %collective-permute-start.6 = (bf16[2,128,128]{2,0,1:T(2,128)(2,1)S(1)}, bf16[2,128,128]{2,0,1:T(2,128)(2,1)S(1)}, u32[]{:S(2)}, u32[]{:S(2)}) collective-permute-start(bf16[2,128,128]{2,0,1:T(2,128)(2,1)S(1)} %bitcast.207), channel_id=1, source_target_pairs={{384,0},{392,8},{400,16},{408,24},{416,32},{424,40},{432,48},{440,... | collective-permute-start | bytes 196616 | tf_op jit(solution)/shard_map/ppermute | solution.py:14
  194.6 3.6 %collective-permute-start.7 = (bf16[2,128,128]{2,0,1:T(2,128)(2,1)S(1)}, bf16[2,128,128]{2,0,1:T(2,128)(2,1)S(1)}, u32[]{:S(2)}, u32[]{:S(2)}) collective-permute-start(bf16[2,128,128]{2,0,1:T(2,128)(2,1)S(1)} %bitcast.206), channel_id=1, source_target_pairs={{448,0},{456,8},{464,16},{472,24},{480,32},{488,40},{496,48},{504,... | collective-permute-start | bytes 196616 | tf_op jit(solution)/shard_map/ppermute | solution.py:14
  198.4 4.3 %collective-permute-start.17 = (bf16[2,128,128]{2,0,1:T(2,128)(2,1)S(1)}, bf16[2,128,128]{2,0,1:T(2,128)(2,1)S(1)}, u32[]{:S(2)}, u32[]{:S(2)}) collective-permute-start(bf16[2,128,128]{2,0,1:T(2,128)(2,1)S(1)} %bitcast.204), channel_id=1, source_target_pairs={{64,0},{72,8},{80,16},{88,24},{96,32},{104,40},{112,48},{120,56},{... | collective-permute-start | bytes 196616 | tf_op jit(solution)/shard_map/ppermute | solution.py:14
  202.8 7.3 %collective-permute-start.18 = (bf16[2,128,128]{2,0,1:T(2,128)(2,1)S(1)}, bf16[2,128,128]{2,0,1:T(2,128)(2,1)S(1)}, u32[]{:S(2)}, u32[]{:S(2)}) collective-permute-start(bf16[2,128,128]{2,0,1:T(2,128)(2,1)S(1)} %bitcast.203), channel_id=1, source_target_pairs={{128,0},{136,8},{144,16},{152,24},{160,32},{168,40},{176,48},{184,... | collective-permute-start | bytes 196616 | tf_op jit(solution)/shard_map/ppermute | solution.py:14
  210.2 6.0 %collective-permute-start.19 = (bf16[2,128,128]{2,0,1:T(2,128)(2,1)S(1)}, bf16[2,128,128]{2,0,1:T(2,128)(2,1)S(1)}, u32[]{:S(2)}, u32[]{:S(2)}) collective-permute-start(bf16[2,128,128]{2,0,1:T(2,128)(2,1)S(1)} %bitcast.202), channel_id=1, source_target_pairs={{192,0},{200,8},{208,16},{216,24},{224,32},{232,40},{240,48},{248,... | collective-permute-start | bytes 196616 | tf_op jit(solution)/shard_map/ppermute | solution.py:14
  216.3 5.6 %collective-permute-start.20 = (bf16[2,128,128]{2,0,1:T(2,128)(2,1)S(1)}, bf16[2,128,128]{2,0,1:T(2,128)(2,1)S(1)}, u32[]{:S(2)}, u32[]{:S(2)}) collective-permute-start(bf16[2,128,128]{2,0,1:T(2,128)(2,1)S(1)} %bitcast.201), channel_id=1, source_target_pairs={{256,0},{264,8},{272,16},{280,24},{288,32},{296,40},{304,48},{312,... | collective-permute-start | bytes 196616 | tf_op jit(solution)/shard_map/ppermute | solution.py:14
  221.9 0.8 convolution_convert_fusion.1
  223.1 0.8 convolution_bitcast_fusion.1
  224.6 1.4 reshape.157
  226.1 6.0 %collective-permute-start.21 = (bf16[2,128,128]{2,0,1:T(2,128)(2,1)S(1)}, bf16[2,128,128]{2,0,1:T(2,128)(2,1)S(1)}, u32[]{:S(2)}, u32[]{:S(2)}) collective-permute-start(bf16[2,128,128]{2,0,1:T(2,128)(2,1)S(1)} %bitcast.200), channel_id=1, source_target_pairs={{320,0},{328,8},{336,16},{344,24},{352,32},{360,40},{368,48},{376,... | collective-permute-start | bytes 196616 | tf_op jit(solution)/shard_map/ppermute | solution.py:14
  232.1 6.1 %collective-permute-start.22 = (bf16[2,128,128]{2,0,1:T(2,128)(2,1)S(1)}, bf16[2,128,128]{2,0,1:T(2,128)(2,1)S(1)}, u32[]{:S(2)}, u32[]{:S(2)}) collective-permute-start(bf16[2,128,128]{2,0,1:T(2,128)(2,1)S(1)} %bitcast.199), channel_id=1, source_target_pairs={{384,0},{392,8},{400,16},{408,24},{416,32},{424,40},{432,48},{440,... | collective-permute-start | bytes 196616 | tf_op jit(solution)/shard_map/ppermute | solution.py:14
  238.3 5.7 %collective-permute-start.23 = (bf16[2,128,128]{2,0,1:T(2,128)(2,1)S(1)}, bf16[2,128,128]{2,0,1:T(2,128)(2,1)S(1)}, u32[]{:S(2)}, u32[]{:S(2)}) collective-permute-start(bf16[2,128,128]{2,0,1:T(2,128)(2,1)S(1)} %bitcast.198), channel_id=1, source_target_pairs={{448,0},{456,8},{464,16},{472,24},{480,32},{488,40},{496,48},{504,... | collective-permute-start | bytes 196616 | tf_op jit(solution)/shard_map/ppermute | solution.py:14
  244.4 2.2 collective-permute-done.23
  246.7 0.8 convolution_convert_fusion
  247.9 0.8 convolution_bitcast_fusion
  249.4 1.4 reshape.159
  250.8 6.2 %reduce-scatter.9.cloned.1.call-done = f32[64,2048]{1,0:T(8,128)} async-done(((f32[128,2048]{1,0:T(8,128)}), f32[64,2048]{1,0:T(8,128)}) %reduce-scatter.9.cloned.1.call-update) | async-done | bytes 524304
  257.0 1.4 reshape.158
  258.4 36.8 %reduce-scatter.11.cloned.1.call-done = f32[64,2048]{1,0:T(8,128)} async-done(((f32[128,2048]{1,0:T(8,128)}), f32[64,2048]{1,0:T(8,128)}) %reduce-scatter.11.cloned.1.call-update) | async-done | bytes 524304
  295.2 1.4 reshape.160
  297.0 0.9 copy.133
  (95 shorter events, 8.2 us)
Async XLA Ops:
  7.9 14.7 %all-to-all-start.1 = ((s32[1,8,2]{2,0,1:T(1,128)}), s32[1,8,2]{2,0,1:T(1,128)S(1)}, u32[]{:S(2)}, u32[]{:S(2)}) async-start(s32[1,8,2]{2,0,1:T(1,128)} %copy.118), calls=%async_computation.1 | async-start | bytes 8192 | tf_op jit(solution)/shard_map/all_to_all | solution.py:31
  32.7 22.3 %copy-start = (s32[1,64,8]{1,2,0:T(8,128)S(1)}, s32[1,64,8]{1,2,0:T(8,128)}, u32[]{:S(2)}) copy-start(s32[1,64,8]{1,2,0:T(8,128)} %param.12) | copy-start | bytes 6148
  51.4 134.3 %all-to-all-start.2 = ((bf16[1,8,2,128,128]{4,3,2,0,1:T(8,128)(2,1)}), bf16[1,8,2,128,128]{4,3,2,0,1:T(8,128)(2,1)S(1)}, u32[]{:S(2)}, u32[]{:S(2)}) async-start(bf16[1,8,2,128,128]{4,3,2,0,1:T(8,128)(2,1)} %bitcast.47), calls=%async_computation.2 | async-start | bytes 1048576 | tf_op jit(solution)/shard_map/all_to_all | solution.py:32
  54.9 202.1 %reduce-scatter.9.cloned.1.call-start = ((), (), s32[]{:S(2)}) async-start(), calls=%async_computation.6 | async-start | bytes 1572864
  73.1 35.3 %collective-permute-start.8 = (s32[2]{0:T(128)S(1)}, s32[2]{0:T(128)S(1)}, u32[]{:S(2)}, u32[]{:S(2)}) collective-permute-start(s32[2]{0:T(128)S(1)} %get-tuple-element.28), channel_id=1, source_target_pairs={{0,0},{8,8},{16,16},{24,24},{32,32},{40,40},{48,48},{56,56},{64,64... | collective-permute-start | bytes 32 | tf_op jit(solution)/shard_map/ppermute | solution.py:14
  73.1 37.2 %collective-permute-start.9 = (s32[2]{0:T(128)S(1)}, s32[2]{0:T(128)S(1)}, u32[]{:S(2)}, u32[]{:S(2)}) collective-permute-start(s32[2]{0:T(128)S(1)} %get-tuple-element.27), channel_id=1, source_target_pairs={{64,0},{72,8},{80,16},{88,24},{96,32},{104,40},{112,48},{120,56},{... | collective-permute-start | bytes 32 | tf_op jit(solution)/shard_map/ppermute | solution.py:14
  91.4 24.5 %collective-permute-start.10 = (s32[2]{0:T(128)S(1)}, s32[2]{0:T(128)S(1)}, u32[]{:S(2)}, u32[]{:S(2)}) collective-permute-start(s32[2]{0:T(128)S(1)} %get-tuple-element.26), channel_id=1, source_target_pairs={{128,0},{136,8},{144,16},{152,24},{160,32},{168,40},{176,48},{184,... | collective-permute-start | bytes 32 | tf_op jit(solution)/shard_map/ppermute | solution.py:14
  95.0 26.9 %collective-permute-start.11 = (s32[2]{0:T(128)S(1)}, s32[2]{0:T(128)S(1)}, u32[]{:S(2)}, u32[]{:S(2)}) collective-permute-start(s32[2]{0:T(128)S(1)} %get-tuple-element.25), channel_id=1, source_target_pairs={{192,0},{200,8},{208,16},{216,24},{224,32},{232,40},{240,48},{248,... | collective-permute-start | bytes 32 | tf_op jit(solution)/shard_map/ppermute | solution.py:14
  96.9 25.0 %collective-permute-start.12 = (s32[2]{0:T(128)S(1)}, s32[2]{0:T(128)S(1)}, u32[]{:S(2)}, u32[]{:S(2)}) collective-permute-start(s32[2]{0:T(128)S(1)} %get-tuple-element.24), channel_id=1, source_target_pairs={{256,0},{264,8},{272,16},{280,24},{288,32},{296,40},{304,48},{312,... | collective-permute-start | bytes 32 | tf_op jit(solution)/shard_map/ppermute | solution.py:14
  108.4 15.4 %collective-permute-start.13 = (s32[2]{0:T(128)S(1)}, s32[2]{0:T(128)S(1)}, u32[]{:S(2)}, u32[]{:S(2)}) collective-permute-start(s32[2]{0:T(128)S(1)} %get-tuple-element.23), channel_id=1, source_target_pairs={{320,0},{328,8},{336,16},{344,24},{352,32},{360,40},{368,48},{376,... | collective-permute-start | bytes 32 | tf_op jit(solution)/shard_map/ppermute | solution.py:14
  110.4 19.6 %collective-permute-start.14 = (s32[2]{0:T(128)S(1)}, s32[2]{0:T(128)S(1)}, u32[]{:S(2)}, u32[]{:S(2)}) collective-permute-start(s32[2]{0:T(128)S(1)} %get-tuple-element.22), channel_id=1, source_target_pairs={{384,0},{392,8},{400,16},{408,24},{416,32},{424,40},{432,48},{440,... | collective-permute-start | bytes 32 | tf_op jit(solution)/shard_map/ppermute | solution.py:14
  115.9 22.0 %collective-permute-start.15 = (s32[2]{0:T(128)S(1)}, s32[2]{0:T(128)S(1)}, u32[]{:S(2)}, u32[]{:S(2)}) collective-permute-start(s32[2]{0:T(128)S(1)} %get-tuple-element.21), channel_id=1, source_target_pairs={{448,0},{456,8},{464,16},{472,24},{480,32},{488,40},{496,48},{504,... | collective-permute-start | bytes 32 | tf_op jit(solution)/shard_map/ppermute | solution.py:14
  121.9 19.7 %collective-permute-start.24 = (s32[2]{0:T(128)S(1)}, s32[2]{0:T(128)S(1)}, u32[]{:S(2)}, u32[]{:S(2)}) collective-permute-start(s32[2]{0:T(128)S(1)} %get-tuple-element.36), channel_id=1, source_target_pairs={{0,0},{8,8},{16,16},{24,24},{32,32},{40,40},{48,48},{56,56},{64,64... | collective-permute-start | bytes 32 | tf_op jit(solution)/shard_map/ppermute | solution.py:14
  121.9 28.7 %collective-permute-start.25 = (s32[2]{0:T(128)S(1)}, s32[2]{0:T(128)S(1)}, u32[]{:S(2)}, u32[]{:S(2)}) collective-permute-start(s32[2]{0:T(128)S(1)} %get-tuple-element.35), channel_id=1, source_target_pairs={{64,0},{72,8},{80,16},{88,24},{96,32},{104,40},{112,48},{120,56},{... | collective-permute-start | bytes 32 | tf_op jit(solution)/shard_map/ppermute | solution.py:14
  123.9 32.9 %collective-permute-start.26 = (s32[2]{0:T(128)S(1)}, s32[2]{0:T(128)S(1)}, u32[]{:S(2)}, u32[]{:S(2)}) collective-permute-start(s32[2]{0:T(128)S(1)} %get-tuple-element.34), channel_id=1, source_target_pairs={{128,0},{136,8},{144,16},{152,24},{160,32},{168,40},{176,48},{184,... | collective-permute-start | bytes 32 | tf_op jit(solution)/shard_map/ppermute | solution.py:14
  130.0 28.7 %collective-permute-start.27 = (s32[2]{0:T(128)S(1)}, s32[2]{0:T(128)S(1)}, u32[]{:S(2)}, u32[]{:S(2)}) collective-permute-start(s32[2]{0:T(128)S(1)} %get-tuple-element.33), channel_id=1, source_target_pairs={{192,0},{200,8},{208,16},{216,24},{224,32},{232,40},{240,48},{248,... | collective-permute-start | bytes 32 | tf_op jit(solution)/shard_map/ppermute | solution.py:14
  137.8 20.9 %collective-permute-start.28 = (s32[2]{0:T(128)S(1)}, s32[2]{0:T(128)S(1)}, u32[]{:S(2)}, u32[]{:S(2)}) collective-permute-start(s32[2]{0:T(128)S(1)} %get-tuple-element.32), channel_id=1, source_target_pairs={{256,0},{264,8},{272,16},{280,24},{288,32},{296,40},{304,48},{312,... | collective-permute-start | bytes 32 | tf_op jit(solution)/shard_map/ppermute | solution.py:14
  141.6 17.1 %collective-permute-start.29 = (s32[2]{0:T(128)S(1)}, s32[2]{0:T(128)S(1)}, u32[]{:S(2)}, u32[]{:S(2)}) collective-permute-start(s32[2]{0:T(128)S(1)} %get-tuple-element.31), channel_id=1, source_target_pairs={{320,0},{328,8},{336,16},{344,24},{352,32},{360,40},{368,48},{376,... | collective-permute-start | bytes 32 | tf_op jit(solution)/shard_map/ppermute | solution.py:14
  150.6 9.4 %collective-permute-start.30 = (s32[2]{0:T(128)S(1)}, s32[2]{0:T(128)S(1)}, u32[]{:S(2)}, u32[]{:S(2)}) collective-permute-start(s32[2]{0:T(128)S(1)} %get-tuple-element.30), channel_id=1, source_target_pairs={{384,0},{392,8},{400,16},{408,24},{416,32},{424,40},{432,48},{440,... | collective-permute-start | bytes 32 | tf_op jit(solution)/shard_map/ppermute | solution.py:14
  156.8 7.6 %collective-permute-start.31 = (s32[2]{0:T(128)S(1)}, s32[2]{0:T(128)S(1)}, u32[]{:S(2)}, u32[]{:S(2)}) collective-permute-start(s32[2]{0:T(128)S(1)} %get-tuple-element.29), channel_id=1, source_target_pairs={{448,0},{456,8},{464,16},{472,24},{480,32},{488,40},{496,48},{504,... | collective-permute-start | bytes 32 | tf_op jit(solution)/shard_map/ppermute | solution.py:14
  164.5 22.0 %collective-permute-start = (bf16[2,128,128]{2,0,1:T(2,128)(2,1)S(1)}, bf16[2,128,128]{2,0,1:T(2,128)(2,1)S(1)}, u32[]{:S(2)}, u32[]{:S(2)}) collective-permute-start(bf16[2,128,128]{2,0,1:T(2,128)(2,1)S(1)} %bitcast.213), channel_id=1, source_target_pairs={{0,0},{8,8},{16,16},{24,24},{32,32},{40,40},{48,48},{56,56},{64,64... | collective-permute-start | bytes 196616 | tf_op jit(solution)/shard_map/ppermute | solution.py:14
  164.6 26.3 %collective-permute-start.1 = (bf16[2,128,128]{2,0,1:T(2,128)(2,1)S(1)}, bf16[2,128,128]{2,0,1:T(2,128)(2,1)S(1)}, u32[]{:S(2)}, u32[]{:S(2)}) collective-permute-start(bf16[2,128,128]{2,0,1:T(2,128)(2,1)S(1)} %bitcast.212), channel_id=1, source_target_pairs={{64,0},{72,8},{80,16},{88,24},{96,32},{104,40},{112,48},{120,56},{... | collective-permute-start | bytes 196616 | tf_op jit(solution)/shard_map/ppermute | solution.py:14
  167.1 27.5 %collective-permute-start.2 = (bf16[2,128,128]{2,0,1:T(2,128)(2,1)S(1)}, bf16[2,128,128]{2,0,1:T(2,128)(2,1)S(1)}, u32[]{:S(2)}, u32[]{:S(2)}) collective-permute-start(bf16[2,128,128]{2,0,1:T(2,128)(2,1)S(1)} %bitcast.211), channel_id=1, source_target_pairs={{128,0},{136,8},{144,16},{152,24},{160,32},{168,40},{176,48},{184,... | collective-permute-start | bytes 196616 | tf_op jit(solution)/shard_map/ppermute | solution.py:14
  170.8 27.5 %collective-permute-start.3 = (bf16[2,128,128]{2,0,1:T(2,128)(2,1)S(1)}, bf16[2,128,128]{2,0,1:T(2,128)(2,1)S(1)}, u32[]{:S(2)}, u32[]{:S(2)}) collective-permute-start(bf16[2,128,128]{2,0,1:T(2,128)(2,1)S(1)} %bitcast.210), channel_id=1, source_target_pairs={{192,0},{200,8},{208,16},{216,24},{224,32},{232,40},{240,48},{248,... | collective-permute-start | bytes 196616 | tf_op jit(solution)/shard_map/ppermute | solution.py:14
  176.5 21.9 %collective-permute-start.4 = (bf16[2,128,128]{2,0,1:T(2,128)(2,1)S(1)}, bf16[2,128,128]{2,0,1:T(2,128)(2,1)S(1)}, u32[]{:S(2)}, u32[]{:S(2)}) collective-permute-start(bf16[2,128,128]{2,0,1:T(2,128)(2,1)S(1)} %bitcast.209), channel_id=1, source_target_pairs={{256,0},{264,8},{272,16},{280,24},{288,32},{296,40},{304,48},{312,... | collective-permute-start | bytes 196616 | tf_op jit(solution)/shard_map/ppermute | solution.py:14
  185.8 36.1 %copy-start.3 = (s32[1,1,4]{2,1,0:T(1,128)S(1)}, s32[1,1,4]{2,1,0:T(1,128)}, u32[]{:S(2)}) copy-start(s32[1,1,4]{2,1,0:T(1,128)} %param.13) | copy-start | bytes 52
  186.4 16.4 %collective-permute-start.5 = (bf16[2,128,128]{2,0,1:T(2,128)(2,1)S(1)}, bf16[2,128,128]{2,0,1:T(2,128)(2,1)S(1)}, u32[]{:S(2)}, u32[]{:S(2)}) collective-permute-start(bf16[2,128,128]{2,0,1:T(2,128)(2,1)S(1)} %bitcast.208), channel_id=1, source_target_pairs={{320,0},{328,8},{336,16},{344,24},{352,32},{360,40},{368,48},{376,... | collective-permute-start | bytes 196616 | tf_op jit(solution)/shard_map/ppermute | solution.py:14
  190.9 19.3 %collective-permute-start.6 = (bf16[2,128,128]{2,0,1:T(2,128)(2,1)S(1)}, bf16[2,128,128]{2,0,1:T(2,128)(2,1)S(1)}, u32[]{:S(2)}, u32[]{:S(2)}) collective-permute-start(bf16[2,128,128]{2,0,1:T(2,128)(2,1)S(1)} %bitcast.207), channel_id=1, source_target_pairs={{384,0},{392,8},{400,16},{408,24},{416,32},{424,40},{432,48},{440,... | collective-permute-start | bytes 196616 | tf_op jit(solution)/shard_map/ppermute | solution.py:14
  194.6 21.6 %collective-permute-start.7 = (bf16[2,128,128]{2,0,1:T(2,128)(2,1)S(1)}, bf16[2,128,128]{2,0,1:T(2,128)(2,1)S(1)}, u32[]{:S(2)}, u32[]{:S(2)}) collective-permute-start(bf16[2,128,128]{2,0,1:T(2,128)(2,1)S(1)} %bitcast.206), channel_id=1, source_target_pairs={{448,0},{456,8},{464,16},{472,24},{480,32},{488,40},{496,48},{504,... | collective-permute-start | bytes 196616 | tf_op jit(solution)/shard_map/ppermute | solution.py:14
  198.4 27.7 %collective-permute-start.16 = (bf16[2,128,128]{2,0,1:T(2,128)(2,1)S(1)}, bf16[2,128,128]{2,0,1:T(2,128)(2,1)S(1)}, u32[]{:S(2)}, u32[]{:S(2)}) collective-permute-start(bf16[2,128,128]{2,0,1:T(2,128)(2,1)S(1)} %bitcast.205), channel_id=1, source_target_pairs={{0,0},{8,8},{16,16},{24,24},{32,32},{40,40},{48,48},{56,56},{64,64... | collective-permute-start | bytes 196616 | tf_op jit(solution)/shard_map/ppermute | solution.py:14
  198.4 33.7 %collective-permute-start.17 = (bf16[2,128,128]{2,0,1:T(2,128)(2,1)S(1)}, bf16[2,128,128]{2,0,1:T(2,128)(2,1)S(1)}, u32[]{:S(2)}, u32[]{:S(2)}) collective-permute-start(bf16[2,128,128]{2,0,1:T(2,128)(2,1)S(1)} %bitcast.204), channel_id=1, source_target_pairs={{64,0},{72,8},{80,16},{88,24},{96,32},{104,40},{112,48},{120,56},{... | collective-permute-start | bytes 196616 | tf_op jit(solution)/shard_map/ppermute | solution.py:14
  202.8 35.5 %collective-permute-start.18 = (bf16[2,128,128]{2,0,1:T(2,128)(2,1)S(1)}, bf16[2,128,128]{2,0,1:T(2,128)(2,1)S(1)}, u32[]{:S(2)}, u32[]{:S(2)}) collective-permute-start(bf16[2,128,128]{2,0,1:T(2,128)(2,1)S(1)} %bitcast.203), channel_id=1, source_target_pairs={{128,0},{136,8},{144,16},{152,24},{160,32},{168,40},{176,48},{184,... | collective-permute-start | bytes 196616 | tf_op jit(solution)/shard_map/ppermute | solution.py:14
  210.2 33.9 %collective-permute-start.19 = (bf16[2,128,128]{2,0,1:T(2,128)(2,1)S(1)}, bf16[2,128,128]{2,0,1:T(2,128)(2,1)S(1)}, u32[]{:S(2)}, u32[]{:S(2)}) collective-permute-start(bf16[2,128,128]{2,0,1:T(2,128)(2,1)S(1)} %bitcast.202), channel_id=1, source_target_pairs={{192,0},{200,8},{208,16},{216,24},{224,32},{232,40},{240,48},{248,... | collective-permute-start | bytes 196616 | tf_op jit(solution)/shard_map/ppermute | solution.py:14
  216.3 27.9 %collective-permute-start.20 = (bf16[2,128,128]{2,0,1:T(2,128)(2,1)S(1)}, bf16[2,128,128]{2,0,1:T(2,128)(2,1)S(1)}, u32[]{:S(2)}, u32[]{:S(2)}) collective-permute-start(bf16[2,128,128]{2,0,1:T(2,128)(2,1)S(1)} %bitcast.201), channel_id=1, source_target_pairs={{256,0},{264,8},{272,16},{280,24},{288,32},{296,40},{304,48},{312,... | collective-permute-start | bytes 196616 | tf_op jit(solution)/shard_map/ppermute | solution.py:14
  221.9 1.2 copy-start.1
  226.0 69.2 %reduce-scatter.11.cloned.1.call-start = ((), (), s32[]{:S(2)}) async-start(), calls=%async_computation.7 | async-start | bytes 1572864
  226.1 18.1 %collective-permute-start.21 = (bf16[2,128,128]{2,0,1:T(2,128)(2,1)S(1)}, bf16[2,128,128]{2,0,1:T(2,128)(2,1)S(1)}, u32[]{:S(2)}, u32[]{:S(2)}) collective-permute-start(bf16[2,128,128]{2,0,1:T(2,128)(2,1)S(1)} %bitcast.200), channel_id=1, source_target_pairs={{320,0},{328,8},{336,16},{344,24},{352,32},{360,40},{368,48},{376,... | collective-permute-start | bytes 196616 | tf_op jit(solution)/shard_map/ppermute | solution.py:14
  232.1 12.2 %collective-permute-start.22 = (bf16[2,128,128]{2,0,1:T(2,128)(2,1)S(1)}, bf16[2,128,128]{2,0,1:T(2,128)(2,1)S(1)}, u32[]{:S(2)}, u32[]{:S(2)}) collective-permute-start(bf16[2,128,128]{2,0,1:T(2,128)(2,1)S(1)} %bitcast.199), channel_id=1, source_target_pairs={{384,0},{392,8},{400,16},{408,24},{416,32},{424,40},{432,48},{440,... | collective-permute-start | bytes 196616 | tf_op jit(solution)/shard_map/ppermute | solution.py:14
  238.3 8.3 %collective-permute-start.23 = (bf16[2,128,128]{2,0,1:T(2,128)(2,1)S(1)}, bf16[2,128,128]{2,0,1:T(2,128)(2,1)S(1)}, u32[]{:S(2)}, u32[]{:S(2)}) collective-permute-start(bf16[2,128,128]{2,0,1:T(2,128)(2,1)S(1)} %bitcast.198), channel_id=1, source_target_pairs={{448,0},{456,8},{464,16},{472,24},{480,32},{488,40},{496,48},{504,... | collective-permute-start | bytes 196616 | tf_op jit(solution)/shard_map/ppermute | solution.py:14
  246.7 1.2 copy-start.2
Sparse Core Ops, SparseCore 0:
  226.2 30.8 reduce-scatter.8
  260.4 34.7 reduce-scatter.10
where the time goes:
time: 309 us; the launch traced here: 305 us
  starting transfers between devices  169 us (55%)
  waiting for transfers between devices  57.9 us (19%)
  between operations  29.9 us (10%)
  blocking collectives  28.8 us (9%)
  local copies, waits for them, and re-layouts  15.5 us (5%)
  matrix products  3.16 us (1%)
    ppermute x32, starting transfers between devices, shifted(): return lax.ppermute(block, axis, route)  158 us
    unnamed x4, waiting for transfers between devices  43.1 us
    all_to_all x1, blocking collectives, body(): lax.all_to_all(x_tiles, 'col', split_axis=1, concat_axis=0, tiled=True)  18.7 us
    all_to_all x1, blocking collectives, body(): lax.all_to_all(x2_cols, 'col', split_axis=1, concat_axis=0, tiled=True)  10.1 us
    unnamed x28, local copies, waits for them, and re-layouts  9.34 us
    ppermute x32, waiting for transfers between devices, shifted(): return lax.ppermute(block, axis, route)  7.91 us
    all_to_all x1, starting transfers between devices, body(): lax.all_to_all(x_cols, 'col', split_axis=1, concat_axis=0, tiled=True)  7.1 us
    all_to_all x1, waiting for transfers between devices, body(): lax.all_to_all(x_cols, 'col', split_axis=1, concat_axis=0, tiled=True)  6.88 us
  transfers between devices with their start and end apart: 36, of which 6 were waited for; matrix products, arithmetic and copies ran while one was open for 5% of the time, Pallas kernels for 0%

commit v1 on v0

v1 whole, which is shorter than its diff:
```python
import functools

import jax
import jax.numpy as jnp
from jax import lax
from jax.experimental import pallas as pl
from jax.experimental.pallas import tpu as pltpu
from jax.sharding import PartitionSpec as P

MESH = pl.DeviceIdType.MESH
BS = 128
NCH = 4
QW = BS // NCH
NT = 4
EXTRA = 16


def one_hot(cond):
    return jnp.where(cond, 1.0, 0.0).astype(jnp.bfloat16)


def iota(shape, dim):
    return lax.broadcasted_iota(jnp.int32, shape, dim)


def kernel(
    sizes, x_hbm, x2_hbm, a_hbm, xc, x2c, req, oc, out_ref, xv, a_raw, a2, pt, w, rs_send, rs_recv,
    own, *rest
):
    n_row, n_col, n_req = sizes
    y_send, y_recv, z_send, z_recv = (rest[i * NCH : (i + 1) * NCH] for i in range(4))
    load_sem, y_ss, y_rs, z_ss, z_rs, r_ss, r_rs = rest[4 * NCH :]
    layer, row, col = (lax.axis_index(a) for a in ("layer", "row", "col"))
    stride = n_row // n_col
    half = own.shape[1]

    loads = [
        pltpu.make_async_copy(x_hbm, xv.at[0], load_sem.at[0]),
        pltpu.make_async_copy(x2_hbm, xv.at[1], load_sem.at[1]),
        pltpu.make_async_copy(a_hbm, a_raw, load_sem.at[2]),
    ]
    for load in loads:
        load.start()

    barrier = pltpu.get_barrier_semaphore()
    peers = [(layer, row, lax.rem(col + d, n_col)) for d in range(1, n_col)]
    peers += [(layer, lax.rem(row + stride * q, n_row), col) for q in range(1, n_req)]
    peers += [(1 - layer, row, col)]
    for peer in peers:
        pl.semaphore_signal(barrier, inc=1, device_id=peer, device_id_type=MESH)

    def rows_sent(j):
        return BS + EXTRA if j == 0 else BS

    def y_copy(j, d):
        n = rows_sent(j)
        to = lax.rem(col + d, n_col)
        return pltpu.make_async_remote_copy(
            src_ref=y_send[j].at[to, pl.ds(0, n)],
            dst_ref=y_recv[j].at[col, pl.ds(0, n)],
            send_sem=y_ss.at[j, d],
            recv_sem=y_rs.at[j, d],
            device_id=(layer, row, to),
            device_id_type=MESH,
        )

    def z_copy(j, q):
        n = rows_sent(j)
        return pltpu.make_async_remote_copy(
            src_ref=z_send[j].at[q, pl.ds(0, n)],
            dst_ref=z_recv[j].at[q, pl.ds(0, n)],
            send_sem=z_ss.at[j, q],
            recv_sem=z_rs.at[j, q],
            device_id=(layer, lax.rem(row - stride * q + n_row, n_row), col),
            device_id_type=MESH,
        )

    def r_copy(j):
        return pltpu.make_async_remote_copy(
            src_ref=rs_send.at[j],
            dst_ref=rs_recv.at[j],
            send_sem=r_ss.at[j],
            recv_sem=r_rs.at[j],
            device_id=(1 - layer, row, col),
            device_id_type=MESH,
        )

    y_order = sorted(range(1, n_col), key=lambda d: abs(2 * d - n_col))
    z_order = sorted(range(1, n_req), key=lambda q: abs(2 * q - n_req))

    loads[0].wait()
    loads[1].wait()
    lane = iota((EXTRA, BS), 1)

    for j in range(NCH):
        src, dst = iota((NT * BS, BS), 0), iota((NT * BS, BS), 1)
        take = one_hot(
            (src // BS == dst // QW) & (lax.rem(src, BS) == lax.rem(dst, QW) + j * QW)
        )

        def build(c, carry, j=j, take=take):
            tiles = jnp.concatenate([xv[0, c, 0], xv[0, c, 1], xv[1, c, 0], xv[1, c, 1]], axis=1)
            chunk = jnp.dot(tiles, take, preferred_element_type=jnp.float32)
            y_send[j][c, 0:BS] = chunk.astype(jnp.bfloat16)
            if j == 0:
                first = jnp.where(lane < QW, xc[0, 0, c], xc[0, 1, c])
                second = jnp.where(lane < 3 * QW, x2c[0, 0, c], x2c[0, 1, c])
                ids = jnp.where(lane < 2 * QW, first, second) >> 3
                y_send[0][c, BS : BS + EXTRA] = ids.astype(jnp.float32).astype(jnp.bfloat16)
            return carry

        lax.fori_loop(0, n_col, build, 0, unroll=True)
        if j == 0:
            pl.semaphore_wait(barrier, len(peers))
        for d in y_order:
            y_copy(j, d).start()
        y_recv[j][col] = y_send[j][col]

    owners = []
    for q in range(n_req):
        reader = lax.rem(row - stride * q + n_row, n_row)
        owners.append(lax.rem(req[0, q, reader], n_col))

    def forward(j):
        for d in y_order:
            y_copy(j, d).wait_recv()
        n = rows_sent(j)
        for q in z_order:
            z_send[j][q, 0:n] = y_recv[j][owners[q], 0:n]
            z_copy(j, q).start()
        z_recv[j][0, 0:n] = y_recv[j][owners[0], 0:n]

    forward(0)

    loads[2].wait()
    group = BS // n_req
    to_row, from_row = iota((BS, BS), 0), iota((BS, BS), 1)
    swap = one_hot(
        (to_row // group == lax.rem(from_row, n_req)) & (lax.rem(to_row, group) == from_row // n_req)
    )

    def regroup(i, carry):
        block = a_raw[pl.ds(pl.multiple_of(i * BS, BS), BS), :]
        moved = jnp.dot(swap, block, preferred_element_type=jnp.float32).astype(jnp.bfloat16)
        for q in range(n_req):
            a2[pl.ds(pl.multiple_of(i * group, group), group), q * BS : (q + 1) * BS] = moved[
                q * group : (q + 1) * group
            ]
        return carry

    lax.fori_loop(0, a_raw.shape[0] // BS, regroup, 0, unroll=4)

    for j in range(1, NCH):
        forward(j)

    target_row = lax.rem(iota((2 * BS, BS), 0), BS) // QW
    target = jnp.where(
        target_row < 2,
        jnp.where(target_row < 1, oc[0, 0, 0], oc[0, 0, 1]),
        jnp.where(target_row < 3, oc[0, 0, 2], oc[0, 0, 3]),
    )
    target = (target >> 3).astype(jnp.float32)
    same_column = lax.rem(iota((2 * BS, BS), 0), QW) == lax.rem(iota((2 * BS, BS), 1), QW)
    same_set = iota((2 * BS, BS), 0) // BS == iota((2 * BS, BS), 1) // (2 * QW)

    def terms(j, start):
        part = jnp.dot(a2[pl.ds(start, half), :], w[...], preferred_element_type=jnp.float32)
        return 4.0 * part[:, :BS] - 3.0 * part[:, BS:]

    own_start = pl.multiple_of(layer * half, half)
    other_start = pl.multiple_of((1 - layer) * half, half)
    for j in range(NCH):
        for q in z_order:
            z_copy(j, q).wait_recv()
        for q in range(n_req):
            if j == 0:
                ids = z_recv[0][q, BS : BS + EXTRA].astype(jnp.float32)[0:1]
                pt[q] = one_hot((ids == target) & same_column & same_set)
            placed = lax.dot_general(
                z_recv[j][q, 0:BS],
                pt[q],
                (((1,), (1,)), ((), ())),
                preferred_element_type=jnp.float32,
            )
            w[q * BS : (q + 1) * BS, :] = placed.astype(jnp.bfloat16)
        rs_send[j] = terms(j, other_start)
        r_copy(j).start()
        own[j] = terms(j, own_start)

    total = jnp.zeros((half, NT * BS), jnp.float32)
    for j in range(NCH):
        r_copy(j).wait_recv()
        summed = (own[j] + rs_recv[j]).astype(jnp.bfloat16)
        src, dst = iota((BS, NT * BS), 0), iota((BS, NT * BS), 1)
        put = one_hot((dst // BS == src // QW) & (lax.rem(dst, BS) == lax.rem(src, QW) + j * QW))
        total = total + jnp.dot(summed, put, preferred_element_type=jnp.float32)
    out_ref[...] = total.astype(jnp.bfloat16)

    for j in range(NCH):
        for d in y_order:
            y_copy(j, d).wait_send()
        for q in z_order:
            z_copy(j, q).wait_send()
        r_copy(j).wait_send()


def body(slab_tiles, x_tiles, x_cols, x2_tiles, x2_cols, requests, out_cols):
    n_row, n_col = lax.axis_size("row"), lax.axis_size("col")
    bs, sr, _, n_req, _ = slab_tiles.shape
    n_out = out_cols.shape[2]
    rows = bs * sr
    half = rows // 2
    vmem, smem = pl.BlockSpec(memory_space=pltpu.VMEM), pl.BlockSpec(memory_space=pltpu.SMEM)
    anywhere = pl.BlockSpec(memory_space=pl.ANY)
    bf16, f32 = jnp.bfloat16, jnp.float32
    out = pl.pallas_call(
        functools.partial(kernel, (n_row, n_col, n_req)),
        name="purify",
        out_shape=jax.ShapeDtypeStruct((half, n_out * bs), bf16),
        in_specs=[anywhere, anywhere, anywhere, smem, smem, smem, smem],
        out_specs=vmem,
        scratch_shapes=[
            pltpu.VMEM((2, n_col, 2, bs, bs), bf16),
            pltpu.VMEM((rows * n_req, bs), bf16),
            pltpu.VMEM((rows, n_req * bs), bf16),
            pltpu.VMEM((n_req, 2 * bs, bs), bf16),
            pltpu.VMEM((n_req * bs, 2 * bs), bf16),
            pltpu.VMEM((NCH, half, bs), f32),
            pltpu.VMEM((NCH, half, bs), f32),
            pltpu.VMEM((NCH, half, bs), f32),
        ]
        + [pltpu.VMEM((n_col, bs + EXTRA, bs), bf16)] * (2 * NCH)
        + [pltpu.VMEM((n_req, bs + EXTRA, bs), bf16)] * (2 * NCH)
        + [
            pltpu.SemaphoreType.DMA((3,)),
            pltpu.SemaphoreType.DMA((NCH, n_col)),
            pltpu.SemaphoreType.DMA((NCH, n_col)),
            pltpu.SemaphoreType.DMA((NCH, n_req)),
            pltpu.SemaphoreType.DMA((NCH, n_req)),
            pltpu.SemaphoreType.DMA((NCH,)),
            pltpu.SemaphoreType.DMA((NCH,)),
        ],
        compiler_params=pltpu.CompilerParams(collective_id=0, has_side_effects=True),
    )(
        x_tiles.reshape(x_tiles.shape[1:]),
        x2_tiles.reshape(x2_tiles.shape[1:]),
        slab_tiles.reshape(rows * n_req, bs),
        jnp.swapaxes(x_cols, 1, 2),
        jnp.swapaxes(x2_cols, 1, 2),
        jnp.swapaxes(requests, 1, 2),
        out_cols,
    )
    return out.reshape(bs // 2, sr, 1, n_out, bs)


def solution(mesh):
    placed = (
        P(None, "row", "layer", None, None),
        P(("layer", "row", "col"), None, None, None, None),
        P(("layer", "row", "col"), None, None),
        P(("layer", "row", "col"), None, None, None, None),
        P(("layer", "row", "col"), None, None),
        P("layer", None, None),
        P("row", "col", None),
    )
    return jax.shard_map(
        body,
        mesh=mesh,
        in_specs=placed,
        out_specs=P("layer", "row", "col", None, None),
        check_vma=False,
    )
```

time: 309 us -> 89.5 us (0.29)
  the two profiles are of different devices: /device:TPU:6 before, /device:TPU:88 now
where the time goes in v1:
time: 89.5 us; the launch traced here: 89.3 us
  Pallas kernels  87.6 us (98%)
  local copies, waits for them, and re-layouts  1.72 us (2%)
    pallas_call x1, Pallas kernels, body(): pl.pallas_call(functools.partial(kernel, (n_row, n_col, n_req)), name='pu...  87.6 us

profile of v1, /device:TPU:88, one launch (start us, length us, event | category | flops | bytes accessed | tf_op | source)
XLA Modules:
  0.0 89.3 jit_solution(16115152321371486883)
XLA Ops:
  0.0 87.6 %purify.1 = bf16[256,512]{1,0:T(8,128)(2,1)} custom-call(bf16[8,2,128,128]{3,2,1,0:T(8,128)(2,1)} %bitcast.8, bf16[8,2,128,128]{3,2,1,0:T(8,128)(2,1)} %bitcast.9, bf16[4096,128]{1,0:T(8,128)(2,1)} %bitcast.7, s32[1,2,8]{2,1,0:T(2,128)} %bitcast.11, s32[1,2,8]{2,1,0:T(2,128)} %bitcast.12, s32[1,8,64]{2,1,0:T(8,128)} %bitcast.10, s32[1,1,4]{2,1,0:T(1,128)} %oc.1), custom_call_target="tpu_custom_call" | custom-call | tf_op jit(solution)/shard_map/purify/pallas_call | solution.py:216
  87.6 1.7 %reshape.15 = bf16[64,4,1,4,128]{4,3,1,0,2:T(4,128)(2,1)} reshape(bf16[256,512]{1,0:T(8,128)(2,1)} %purify.1) | data formatting | bytes 524288 | tf_op jit(solution)/shard_map/reshape | solution.py:253

commit v2 on v1

v2 whole, which is shorter than its diff:
```python
import functools

import jax
import jax.numpy as jnp
from jax import lax
from jax.experimental import pallas as pl
from jax.experimental.pallas import tpu as pltpu
from jax.sharding import PartitionSpec as P

MESH = pl.DeviceIdType.MESH
BS = 128
NCH = 4
QW = BS // NCH
NT = 4
EXTRA = 16
PIECES = (
    (0, 0, 16), (0, 16, 32), (0, 48, 64), (0, 112, 16), (1, 0, 128), (2, 0, 128), (3, 0, 128)
)


def one_hot(cond):
    return jnp.where(cond, 1.0, 0.0).astype(jnp.bfloat16)


def iota(shape, dim):
    return lax.broadcasted_iota(jnp.int32, shape, dim)


IDS = max(p for p in range(len(PIECES)) if PIECES[p][0] == 0)


def piece_rows(p):
    return PIECES[p][2] + (EXTRA if p == IDS else 0)


def kernel(
    sizes, x_hbm, x2_hbm, a_hbm, xc_hbm, x2c_hbm, req_hbm, oc_hbm, out_ref, xc, x2c, req, oc, xv, a_raw, a2, pt, w, rs_send, rs_recv,
    own, total, *rest
):
    n_row, n_col, n_req = sizes
    n_p = len(PIECES)
    y_send, y_recv, z_send, z_recv = (rest[i * n_p : (i + 1) * n_p] for i in range(4))
    load_sem, y_ss, y_rs, z_ss, z_rs, r_ss, r_rs, y_hello, z_hello = rest[4 * n_p :]
    layer, row, col = (lax.axis_index(a) for a in ("layer", "row", "col"))
    stride = n_row // n_col
    place = row // stride
    half = own.shape[1]

    loads = [
        pltpu.make_async_copy(x_hbm, xv.at[0], load_sem.at[0]),
        pltpu.make_async_copy(x2_hbm, xv.at[1], load_sem.at[1]),
        pltpu.make_async_copy(a_hbm, a_raw, load_sem.at[2]),
        pltpu.make_async_copy(req_hbm, req, load_sem.at[3]),
        pltpu.make_async_copy(xc_hbm, xc, load_sem.at[4]),
        pltpu.make_async_copy(x2c_hbm, x2c, load_sem.at[5]),
        pltpu.make_async_copy(oc_hbm, oc, load_sem.at[6]),
    ]
    def y_device(d):
        return (layer, row, lax.rem(col + d, n_col))

    def z_device(q):
        return (layer, lax.rem(row - stride * q + n_row, n_row), col)

    def y_lower(d):
        return col + d >= n_col

    def z_lower(q):
        return q <= place

    barrier = pltpu.get_barrier_semaphore()

    def signal(sem, device):
        pl.semaphore_signal(sem, inc=1, device_id=device, device_id_type=MESH)

    signal(barrier, (1 - layer, row, col))
    for d in range(1, n_col):
        pl.when(jnp.logical_not(y_lower(d)))(functools.partial(signal, barrier, y_device(d)))
    for q in range(1, n_req):
        pl.when(jnp.logical_not(z_lower(q)))(functools.partial(signal, barrier, z_device(q)))

    for load in loads:
        load.start()

    pl.semaphore_wait(barrier, 1 + col + place)
    for q in range(1, n_req):
        pl.when(z_lower(q))(functools.partial(signal, z_hello.at[n_req - q], z_device(q)))
    for d in range(1, n_col):
        pl.when(y_lower(d))(functools.partial(signal, y_hello.at[n_col - d], y_device(d)))

    def y_copy(p, d):
        return pltpu.make_async_remote_copy(
            src_ref=y_send[p].at[lax.rem(col + d, n_col)],
            dst_ref=y_recv[p].at[col],
            send_sem=y_ss.at[p, d],
            recv_sem=y_rs.at[p, d],
            device_id=y_device(d),
            device_id_type=MESH,
        )

    def z_copy(p, q):
        return pltpu.make_async_remote_copy(
            src_ref=z_send[p].at[q],
            dst_ref=z_recv[p].at[q],
            send_sem=z_ss.at[p, q],
            recv_sem=z_rs.at[p, q],
            device_id=z_device(q),
            device_id_type=MESH,
        )

    def r_copy(j):
        return pltpu.make_async_remote_copy(
            src_ref=rs_send.at[j],
            dst_ref=rs_recv.at[j],
            send_sem=r_ss.at[j],
            recv_sem=r_rs.at[j],
            device_id=(1 - layer, row, col),
            device_id_type=MESH,
        )

    y_order = sorted(range(1, n_col), key=lambda d: abs(2 * d - n_col))
    z_order = sorted(range(1, n_req), key=lambda q: abs(2 * q - n_req))

    def heard(sem, *copies):
        pl.semaphore_wait(sem, 1)
        for copy in copies:
            copy.start()

    def build(p):
        j, at, n = PIECES[p]
        src, dst = iota((NT * BS, BS), 0), iota((NT * BS, BS), 1)
        take = one_hot(
            (src // BS == dst // QW) & (lax.rem(src, BS) == lax.rem(dst, QW) + j * QW)
        )
        group = n_col if n <= 32 else 1
        for c in range(0, n_col, group):
            tiles = [
                xv[i, c : c + group, u, at : at + n].reshape(group * n, BS)
                for i in range(2)
                for u in range(2)
            ]
            chunk = jnp.dot(
                jnp.concatenate(tiles, axis=1), take, preferred_element_type=jnp.float32
            )
            y_send[p][c : c + group, 0:n] = chunk.astype(jnp.bfloat16).reshape(group, n, BS)
        if p == IDS:
            lane = iota((EXTRA, BS), 1)
            for c in range(n_col):
                first = jnp.where(lane < QW, xc[0, 0, c], xc[0, 1, c])
                second = jnp.where(lane < 3 * QW, x2c[0, 0, c], x2c[0, 1, c])
                ids = jnp.where(lane < 2 * QW, first, second) >> 3
                y_send[p][c, n : n + EXTRA] = ids.astype(jnp.float32).astype(jnp.bfloat16)

    def send(p):
        for d in y_order:
            if p == 0:
                pl.when(y_lower(d))(y_copy(p, d).start)
            else:
                y_copy(p, d).start()
        if p == 0:
            for d in range(1, n_col):
                wait = functools.partial(heard, y_hello.at[d], y_copy(p, d))
                pl.when(jnp.logical_not(y_lower(d)))(wait)
        y_recv[p][col] = y_send[p][col]

    def forward(p):
        for d in y_order:
            y_copy(p, d).wait_recv()
        for q in z_order:
            z_send[p][q] = y_recv[p][owners[q]]
            if p <= 1:
                pl.when(z_lower(q))(z_copy(p, q).start)
            else:
                z_copy(p, q).start()
        z_recv[p][0] = y_recv[p][owners[0]]

    def upper(pieces, steps, wait):
        for k in steps:
            q = n_req - k
            copies = [z_copy(p, q) for p in pieces]

            def go(q=q, copies=copies):
                if wait:
                    heard(z_hello.at[q], *copies)
                else:
                    for copy in copies:
                        copy.start()

            pl.when(jnp.logical_not(z_lower(q)))(go)

    loads[0].wait()
    loads[1].wait()
    build(0)
    send(0)
    build(1)
    send(1)
    build(2)
    send(2)
    for load in loads[3:]:
        load.wait()
    owners = []
    for q in range(n_req):
        reader = lax.rem(row - stride * q + n_row, n_row)
        owners.append(lax.rem(req[0, q, reader], n_col))

    build(3)
    send(3)

    group = BS // n_req
    to_row, from_row = iota((BS, BS), 0), iota((BS, BS), 1)
    swap = one_hot(
        (to_row // group == lax.rem(from_row, n_req)) & (lax.rem(to_row, group) == from_row // n_req)
    )

    def regroup(i, carry):
        block = a_raw[pl.ds(pl.multiple_of(i * BS, BS), BS), :]
        moved = jnp.dot(swap, block, preferred_element_type=jnp.float32).astype(jnp.bfloat16)
        for q in range(n_req):
            a2[pl.ds(pl.multiple_of(i * group, group), group), q * BS : (q + 1) * BS] = moved[
                q * group : (q + 1) * group
            ]
        return carry

    forward(0)
    upper((0,), (1, 2), True)
    build(4)
    send(4)
    forward(1)
    upper((1,), (1, 2), False)
    upper((0, 1), (3, 4), True)
    loads[2].wait()
    lax.fori_loop(0, a_raw.shape[0] // BS, regroup, 0, unroll=4)
    upper((0, 1), range(5, n_req), True)
    forward(2)
    build(5)
    send(5)
    forward(3)
    build(6)
    send(6)
    for p in range(4, n_p):
        forward(p)

    target_row = lax.rem(iota((2 * BS, BS), 0), BS) // QW
    target = jnp.where(
        target_row < 2,
        jnp.where(target_row < 1, oc[0, 0, 0], oc[0, 0, 1]),
        jnp.where(target_row < 3, oc[0, 0, 2], oc[0, 0, 3]),
    )
    target = (target >> 3).astype(jnp.float32)
    same_column = lax.rem(iota((2 * BS, BS), 0), QW) == lax.rem(iota((2 * BS, BS), 1), QW)
    same_set = iota((2 * BS, BS), 0) // BS == iota((2 * BS, BS), 1) // (2 * QW)

    def terms(start):
        part = jnp.dot(a2[pl.ds(start, half), :], w[...], preferred_element_type=jnp.float32)
        return 4.0 * part[:, :BS] - 3.0 * part[:, BS:]

    def finish(j):
        r_copy(j).wait_recv()
        summed = (own[j] + rs_recv[j]).astype(jnp.bfloat16)
        src, dst = iota((BS, NT * BS), 0), iota((BS, NT * BS), 1)
        put = one_hot((dst // BS == src // QW) & (lax.rem(dst, BS) == lax.rem(src, QW) + j * QW))
        moved = jnp.dot(summed, put, preferred_element_type=jnp.float32)
        if j == 0:
            total[...] = moved
        elif j < NCH - 1:
            total[...] += moved
        else:
            out_ref[...] = (total[...] + moved).astype(jnp.bfloat16)

    own_start = pl.multiple_of(layer * half, half)
    other_start = pl.multiple_of((1 - layer) * half, half)
    for j in range(NCH):
        mine = [p for p in range(n_p) if PIECES[p][0] == j]
        for q in (0, *reversed(z_order)):
            if q:
                for p in mine:
                    z_copy(p, q).wait_recv()
            if j == 0:
                n = PIECES[IDS][2]
                ids = z_recv[IDS][q, n : n + EXTRA].astype(jnp.float32)[0:1]
                pt[q] = one_hot((ids == target) & same_column & same_set)
            tiles = [z_recv[p][q, 0 : PIECES[p][2]] for p in mine]
            placed = lax.dot_general(
                tiles[0] if len(tiles) == 1 else jnp.concatenate(tiles, axis=0),
                pt[q],
                (((1,), (1,)), ((), ())),
                preferred_element_type=jnp.float32,
            )
            w[q * BS : (q + 1) * BS, :] = placed.astype(jnp.bfloat16)
        rs_send[j] = terms(other_start)
        r_copy(j).start()
        own[j] = terms(own_start)
        if j:
            finish(j - 1)
    finish(NCH - 1)

    for p in range(n_p):
        for d in y_order:
            y_copy(p, d).wait_send()
        for q in z_order:
            z_copy(p, q).wait_send()
    for j in range(NCH):
        r_copy(j).wait_send()


def body(slab_tiles, x_tiles, x_cols, x2_tiles, x2_cols, requests, out_cols):
    n_row, n_col = lax.axis_size("row"), lax.axis_size("col")
    bs, sr, _, n_req, _ = slab_tiles.shape
    n_out = out_cols.shape[2]
    rows = bs * sr
    half, n_p = rows // 2, len(PIECES)
    vmem = pl.BlockSpec(memory_space=pltpu.VMEM)
    anywhere = pl.BlockSpec(memory_space=pl.ANY)
    bf16, f32 = jnp.bfloat16, jnp.float32
    out = pl.pallas_call(
        functools.partial(kernel, (n_row, n_col, n_req)),
        name="purify",
        out_shape=jax.ShapeDtypeStruct((half, n_out * bs), bf16),
        in_specs=[anywhere] * 7,
        out_specs=vmem,
        scratch_shapes=[
            pltpu.SMEM((1, 2, n_col), jnp.int32),
            pltpu.SMEM((1, 2, n_col), jnp.int32),
            pltpu.SMEM((1, n_req, n_row), jnp.int32),
            pltpu.SMEM((1, 1, n_out), jnp.int32),
            pltpu.VMEM((2, n_col, 2, bs, bs), bf16),
            pltpu.VMEM((rows * n_req, bs), bf16),
            pltpu.VMEM((rows, n_req * bs), bf16),
            pltpu.VMEM((n_req, 2 * bs, bs), bf16),
            pltpu.VMEM((n_req * bs, 2 * bs), bf16),
            pltpu.VMEM((NCH, half, bs), f32),
            pltpu.VMEM((NCH, half, bs), f32),
            pltpu.VMEM((NCH, half, bs), f32),
        ]
        + [pltpu.VMEM((half, n_out * bs), f32)]
        + [pltpu.VMEM((n_col, piece_rows(p), bs), bf16) for p in range(n_p)] * 2
        + [pltpu.VMEM((n_req, piece_rows(p), bs), bf16) for p in range(n_p)] * 2
        + [
            pltpu.SemaphoreType.DMA((7,)),
            pltpu.SemaphoreType.DMA((n_p, n_col)),
            pltpu.SemaphoreType.DMA((n_p, n_col)),
            pltpu.SemaphoreType.DMA((n_p, n_req)),
            pltpu.SemaphoreType.DMA((n_p, n_req)),
            pltpu.SemaphoreType.DMA((NCH,)),
            pltpu.SemaphoreType.DMA((NCH,)),
            pltpu.SemaphoreType.REGULAR((n_col,)),
            pltpu.SemaphoreType.REGULAR((n_req,)),
        ],
        compiler_params=pltpu.CompilerParams(collective_id=0, has_side_effects=True),
    )(
        x_tiles.reshape(x_tiles.shape[1:]),
        x2_tiles.reshape(x2_tiles.shape[1:]),
        slab_tiles.reshape(rows * n_req, bs),
        jnp.swapaxes(x_cols, 1, 2),
        jnp.swapaxes(x2_cols, 1, 2),
        jnp.swapaxes(requests, 1, 2),
        out_cols,
    )
    return out.reshape(bs // 2, sr, 1, n_out, bs)


def solution(mesh):
    placed = (
        P(None, "row", "layer", None, None),
        P(("layer", "row", "col"), None, None, None, None),
        P(("layer", "row", "col"), None, None),
        P(("layer", "row", "col"), None, None, None, None),
        P(("layer", "row", "col"), None, None),
        P("layer", None, None),
        P("row", "col", None),
    )
    return jax.shard_map(
        body,
        mesh=mesh,
        in_specs=placed,
        out_specs=P("layer", "row", "col", None, None),
        check_vma=False,
    )
```

time: 89.5 us -> 86.1 us (0.962)
  the two profiles are of different devices: /device:TPU:88 before, /device:TPU:6 now
where the time goes in v2:
time: 86.1 us; the launch traced here: 86 us
  Pallas kernels  84.2 us (98%)
  local copies, waits for them, and re-layouts  1.72 us (2%)
    pallas_call x1, Pallas kernels, body(): pl.pallas_call(functools.partial(kernel, (n_row, n_col, n_req)), name='pu...  84.2 us

profile of v2, /device:TPU:6, one launch (start us, length us, event | category | flops | bytes accessed | tf_op | source)
XLA Modules:
  0.0 86.0 jit_solution(8725032707470279690)
XLA Ops:
  0.0 84.2 %purify.1 = bf16[256,512]{1,0:T(8,128)(2,1)} custom-call(bf16[8,2,128,128]{3,2,1,0:T(8,128)(2,1)} %bitcast.8, bf16[8,2,128,128]{3,2,1,0:T(8,128)(2,1)} %bitcast.9, bf16[4096,128]{1,0:T(8,128)(2,1)} %bitcast.7, s32[1,2,8]{2,1,0:T(2,128)} %bitcast.11, s32[1,2,8]{2,1,0:T(2,128)} %bitcast.12, s32[1,8,64]{2,1,0:T(8,128)} %bitcast.10, s32[1,1,4]{2,1,0:T(1,128)} %oc_hbm.1), custom_call_target="tpu_custom_call" | custom-call | tf_op jit(solution)/shard_map/purify/pallas_call | solution.py:314
  84.2 1.7 %reshape.15 = bf16[64,4,1,4,128]{4,3,1,0,2:T(4,128)(2,1)} reshape(bf16[256,512]{1,0:T(8,128)(2,1)} %purify.1) | data formatting | bytes 524288 | tf_op jit(solution)/shard_map/reshape | solution.py:358

commit v3 on v2

--- a/solution.py
+++ b/solution.py
@@ -9,12 +9,12 @@
 
 MESH = pl.DeviceIdType.MESH
 BS = 128
-NCH = 4
-QW = BS // NCH
 NT = 4
-EXTRA = 16
+CHUNKS = ((0, 1), (32, 1), (64, 1), (96, 1))
+NCH = len(CHUNKS)
+GROUPS = (1,)
 PIECES = (
-    (0, 0, 16), (0, 16, 32), (0, 48, 64), (0, 112, 16), (1, 0, 128), (2, 0, 128), (3, 0, 128)
+    (0, 0, 16), (0, 16, 32), (0, 48, 64), (0, 112, 16), (-1, 0, 1), (1, 0, 128), (2, 0, 128), (3, 0, 128),
 )
 
 
@@ -26,25 +26,29 @@
     return lax.broadcasted_iota(jnp.int32, shape, dim)
 
 
-IDS = max(p for p in range(len(PIECES)) if PIECES[p][0] == 0)
-
-
-def piece_rows(p):
-    return PIECES[p][2] + (EXTRA if p == IDS else 0)
+IDS = 4
+GATED = 6
+
+
+def piece(p, count):
+    j, _, n = PIECES[p]
+    return pltpu.VMEM((count, n, BS), jnp.bfloat16 if j >= 0 else jnp.float32)
 
 
 def kernel(
-    sizes, x_hbm, x2_hbm, a_hbm, xc_hbm, x2c_hbm, req_hbm, oc_hbm, out_ref, xc, x2c, req, oc, xv, a_raw, a2, pt, w, rs_send, rs_recv,
-    own, total, *rest
+    sizes, x_hbm, x2_hbm, a_hbm, xc_hbm, x2c_hbm, req_hbm, oc_hbm, out_ref, xc, x2c, req, oc, xv,
+    a_raw, a2, pt, w, put, total, *rest
 ):
     n_row, n_col, n_req = sizes
     n_p = len(PIECES)
     y_send, y_recv, z_send, z_recv = (rest[i * n_p : (i + 1) * n_p] for i in range(4))
-    load_sem, y_ss, y_rs, z_ss, z_rs, r_ss, r_rs, y_hello, z_hello = rest[4 * n_p :]
+    rest = rest[4 * n_p :]
+    rs_send, rs_recv, own = (rest[i * NCH : (i + 1) * NCH] for i in range(3))
+    load_sem, y_ss, y_rs, z_ss, z_rs, r_ss, r_rs, y_hello, z_hello = rest[3 * NCH :]
     layer, row, col = (lax.axis_index(a) for a in ("layer", "row", "col"))
     stride = n_row // n_col
     place = row // stride
-    half = own.shape[1]
+    half = total.shape[0]
 
     loads = [
         pltpu.make_async_copy(x_hbm, xv.at[0], load_sem.at[0]),
@@ -109,8 +113,8 @@
 
     def r_copy(j):
         return pltpu.make_async_remote_copy(
-            src_ref=rs_send.at[j],
-            dst_ref=rs_recv.at[j],
+            src_ref=rs_send[j],
+            dst_ref=rs_recv[j],
             send_sem=r_ss.at[j],
             recv_sem=r_rs.at[j],
             device_id=(1 - layer, row, col),
@@ -127,28 +131,37 @@
 
     def build(p):
         j, at, n = PIECES[p]
+        start, groups = CHUNKS[j]
+        wide = BS // groups
         src, dst = iota((NT * BS, BS), 0), iota((NT * BS, BS), 1)
-        take = one_hot(
-            (src // BS == dst // QW) & (lax.rem(src, BS) == lax.rem(dst, QW) + j * QW)
-        )
-        group = n_col if n <= 32 else 1
-        for c in range(0, n_col, group):
-            tiles = [
-                xv[i, c : c + group, u, at : at + n].reshape(group * n, BS)
-                for i in range(2)
-                for u in range(2)
-            ]
-            chunk = jnp.dot(
-                jnp.concatenate(tiles, axis=1), take, preferred_element_type=jnp.float32
-            )
-            y_send[p][c : c + group, 0:n] = chunk.astype(jnp.bfloat16).reshape(group, n, BS)
-        if p == IDS:
-            lane = iota((EXTRA, BS), 1)
-            for c in range(n_col):
-                first = jnp.where(lane < QW, xc[0, 0, c], xc[0, 1, c])
-                second = jnp.where(lane < 3 * QW, x2c[0, 0, c], x2c[0, 1, c])
-                ids = jnp.where(lane < 2 * QW, first, second) >> 3
-                y_send[p][c, n : n + EXTRA] = ids.astype(jnp.float32).astype(jnp.bfloat16)
+        within = lax.rem(dst, wide)
+        width = wide // NT
+        keep = (src // BS == within // width) & (
+            lax.rem(src, BS) == lax.rem(within, width) + start
+        )
+        step = n_col if n <= 32 else 1
+        for c in range(0, n_col, step):
+            chunk = None
+            for g in range(groups):
+                rows = pl.ds(at + g * (BS // groups), n)
+                tiles = [
+                    xv[i, c : c + step, u, rows].reshape(step * n, BS)
+                    for i in range(2)
+                    for u in range(2)
+                ]
+                take = one_hot(keep & (dst // wide == g))
+                part = jnp.dot(
+                    jnp.concatenate(tiles, axis=1), take, preferred_element_type=jnp.float32
+                )
+                chunk = part if chunk is None else chunk + part
+            y_send[p][c : c + step, 0:n] = chunk.astype(jnp.bfloat16).reshape(step, n, BS)
+
+    def build_ids():
+        slot = iota((1, BS), 1) // (BS // NT)
+        for c in range(n_col):
+            first = jnp.where(slot < 1, xc[0, 0, c], xc[0, 1, c])
+            second = jnp.where(slot < 3, x2c[0, 0, c], x2c[0, 1, c])
+            y_send[IDS][c] = jnp.where(slot < 2, first, second).astype(jnp.float32)
 
     def send(p):
         for d in y_order:
@@ -167,7 +180,7 @@
             y_copy(p, d).wait_recv()
         for q in z_order:
             z_send[p][q] = y_recv[p][owners[q]]
-            if p <= 1:
+            if p < GATED:
                 pl.when(z_lower(q))(z_copy(p, q).start)
             else:
                 z_copy(p, q).start()
@@ -204,6 +217,10 @@
 
     build(3)
     send(3)
+    build_ids()
+    send(IDS)
+    build(5)
+    send(5)
 
     group = BS // n_req
     to_row, from_row = iota((BS, BS), 0), iota((BS, BS), 1)
@@ -220,75 +237,125 @@
             ]
         return carry
 
+    near, middle, far = (1, 2), (3, 4), range(5, n_req)
     forward(0)
-    upper((0,), (1, 2), True)
-    build(4)
-    send(4)
+    upper((0,), near, True)
     forward(1)
-    upper((1,), (1, 2), False)
-    upper((0, 1), (3, 4), True)
+    upper((1,), near, False)
+    forward(2)
+    upper((2,), near, False)
+    upper((0, 1, 2), middle, True)
+    forward(3)
+    upper((3,), (*near, *middle), False)
+    build(6)
+    send(6)
+    forward(4)
+    upper((4,), (*near, *middle), False)
+    forward(5)
+    upper((5,), (*near, *middle), False)
+    upper(range(GATED), far, True)
+    for p in range(7, n_p):
+        build(p)
+        send(p)
     loads[2].wait()
     lax.fori_loop(0, a_raw.shape[0] // BS, regroup, 0, unroll=4)
-    upper((0, 1), range(5, n_req), True)
-    forward(2)
-    build(5)
-    send(5)
-    forward(3)
-    build(6)
-    send(6)
-    for p in range(4, n_p):
+
+    def first_put(j):
+        return sum(groups for _, groups in CHUNKS[:j])
+
+    for j, (start, groups) in enumerate(CHUNKS):
+        wide = BS // groups
+        width = wide // NT
+        src, dst = iota((BS, NT * BS), 0), iota((BS, NT * BS), 1)
+        within = lax.rem(src, wide)
+        keep = (dst // BS == within // width) & (
+            lax.rem(dst, BS) == lax.rem(within, width) + start
+        )
+        for g in range(groups):
+            put[first_put(j) + g] = one_hot(keep & (src // wide == g))
+
+    for p in range(GATED, n_p):
         forward(p)
 
-    target_row = lax.rem(iota((2 * BS, BS), 0), BS) // QW
-    target = jnp.where(
-        target_row < 2,
-        jnp.where(target_row < 1, oc[0, 0, 0], oc[0, 0, 1]),
-        jnp.where(target_row < 3, oc[0, 0, 2], oc[0, 0, 3]),
-    )
-    target = (target >> 3).astype(jnp.float32)
-    same_column = lax.rem(iota((2 * BS, BS), 0), QW) == lax.rem(iota((2 * BS, BS), 1), QW)
-    same_set = iota((2 * BS, BS), 0) // BS == iota((2 * BS, BS), 1) // (2 * QW)
-
-    def terms(start):
-        part = jnp.dot(a2[pl.ds(start, half), :], w[...], preferred_element_type=jnp.float32)
-        return 4.0 * part[:, :BS] - 3.0 * part[:, BS:]
+    def placing(groups, ids, g):
+        wide = BS // groups
+        width = wide // NT
+        n = max(2 * wide, BS)
+        to, at = iota((n, BS), 0), iota((n, BS), 1)
+        block = lax.rem(to, wide) // width
+        target = jnp.where(
+            block < 2,
+            jnp.where(block < 1, oc[0, 0, 0], oc[0, 0, 1]),
+            jnp.where(block < 3, oc[0, 0, 2], oc[0, 0, 3]),
+        )
+        target = target.astype(jnp.float32)
+        same_column = lax.rem(to, width) == lax.rem(at, width)
+        same_set = to // wide == lax.rem(at, wide) // (2 * width)
+        return one_hot((ids == target) & same_column & same_set & (at // wide == g))
+
+    def terms(j, start):
+        groups = CHUNKS[j][1]
+        wide = BS // groups
+        n = max(2 * wide, BS)
+        part = jnp.dot(
+            a2[pl.ds(start, half), :], w[:, 0:n], preferred_element_type=jnp.float32
+        )
+        if groups == 1:
+            return 4.0 * part[:, :BS] - 3.0 * part[:, BS:]
+        part = 4.0 * part - 3.0 * pltpu.roll(part, BS - wide, 1)
+        rows = half // groups
+        packed = part[0:rows]
+        lane = iota((rows, BS), 1)
+        for g in range(1, groups):
+            moved = pltpu.roll(part[g * rows : (g + 1) * rows], g * wide, 1)
+            packed = jnp.where(lane // wide == g, moved, packed)
+        return packed
 
     def finish(j):
+        groups = CHUNKS[j][1]
+        rows = half // groups
         r_copy(j).wait_recv()
-        summed = (own[j] + rs_recv[j]).astype(jnp.bfloat16)
-        src, dst = iota((BS, NT * BS), 0), iota((BS, NT * BS), 1)
-        put = one_hot((dst // BS == src // QW) & (lax.rem(dst, BS) == lax.rem(src, QW) + j * QW))
-        moved = jnp.dot(summed, put, preferred_element_type=jnp.float32)
-        if j == 0:
-            total[...] = moved
-        elif j < NCH - 1:
-            total[...] += moved
-        else:
-            out_ref[...] = (total[...] + moved).astype(jnp.bfloat16)
+        summed = (own[j][...] + rs_recv[j][...]).astype(jnp.bfloat16)
+        for g in range(groups):
+            moved = jnp.dot(summed, put[first_put(j) + g], preferred_element_type=jnp.float32)
+            at = slice(g * rows, (g + 1) * rows)
+            if j == 0:
+                total[at] = moved
+            elif j < NCH - 1:
+                total[at] += moved
+            else:
+                out_ref[at] = (total[at] + moved).astype(jnp.bfloat16)
 
     own_start = pl.multiple_of(layer * half, half)
     other_start = pl.multiple_of((1 - layer) * half, half)
     for j in range(NCH):
+        groups = CHUNKS[j][1]
+        n = max(2 * BS // groups, BS)
+        depth = BS // groups
         mine = [p for p in range(n_p) if PIECES[p][0] == j]
-        for q in (0, *reversed(z_order)):
+        kinds = sum(GROUPS[: GROUPS.index(groups)])
+        for q in (0, *z_order):
             if q:
                 for p in mine:
                     z_copy(p, q).wait_recv()
             if j == 0:
-                n = PIECES[IDS][2]
-                ids = z_recv[IDS][q, n : n + EXTRA].astype(jnp.float32)[0:1]
-                pt[q] = one_hot((ids == target) & same_column & same_set)
+                if q:
+                    z_copy(IDS, q).wait_recv()
+                pt[0, q] = placing(groups, z_recv[IDS][q], 0)
             tiles = [z_recv[p][q, 0 : PIECES[p][2]] for p in mine]
-            placed = lax.dot_general(
-                tiles[0] if len(tiles) == 1 else jnp.concatenate(tiles, axis=0),
-                pt[q],
-                (((1,), (1,)), ((), ())),
-                preferred_element_type=jnp.float32,
-            )
-            w[q * BS : (q + 1) * BS, :] = placed.astype(jnp.bfloat16)
-        rs_send[j] = terms(other_start)
+            tile = tiles[0] if len(tiles) == 1 else jnp.concatenate(tiles, axis=0)
+            for g in range(groups):
+                placed = lax.dot_general(
+                    tile,
+                    pt[kinds + g, q, 0:n],
+                    (((1,), (1,)), ((), ())),
+                    preferred_element_type=jnp.float32,
+                )
+                at = q * BS + g * depth
+                w[at : at + depth, 0:n] = placed.astype(jnp.bfloat16)
+        rs_send[j][...] = terms(j, other_start)
         r_copy(j).start()
-        own[j] = terms(own_start)
+        own[j][...] = terms(j, own_start)
         if j:
             finish(j - 1)
     finish(NCH - 1)
@@ -325,15 +392,14 @@
             pltpu.VMEM((2, n_col, 2, bs, bs), bf16),
             pltpu.VMEM((rows * n_req, bs), bf16),
             pltpu.VMEM((rows, n_req * bs), bf16),
-            pltpu.VMEM((n_req, 2 * bs, bs), bf16),
+            pltpu.VMEM((sum(GROUPS), n_req, 2 * bs, bs), bf16),
             pltpu.VMEM((n_req * bs, 2 * bs), bf16),
-            pltpu.VMEM((NCH, half, bs), f32),
-            pltpu.VMEM((NCH, half, bs), f32),
-            pltpu.VMEM((NCH, half, bs), f32),
+            pltpu.VMEM((sum(g for _, g in CHUNKS), bs, NT * bs), bf16),
+            pltpu.VMEM((half, n_out * bs), f32),
         ]
-        + [pltpu.VMEM((half, n_out * bs), f32)]
-        + [pltpu.VMEM((n_col, piece_rows(p), bs), bf16) for p in range(n_p)] * 2
-        + [pltpu.VMEM((n_req, piece_rows(p), bs), bf16) for p in range(n_p)] * 2
+        + [piece(p, n_col) for p in range(n_p)] * 2
+        + [piece(p, n_req) for p in range(n_p)] * 2
+        + [pltpu.VMEM((half // g, bs), f32) for _, g in CHUNKS] * 3
         + [
             pltpu.SemaphoreType.DMA((7,)),
             pltpu.SemaphoreType.DMA((n_p, n_col)),

time: 86.1 us -> 85.3 us (level)
  Pallas kernels: 84.2 us -> 82.9 us
    pallas_call x1, Pallas kernels: 84.2 us -> 82.9 us  [body(): pl.pallas_call(functools.partial(kernel, (n_row, n_col, n_req)), name='pu...]
where the time goes in v3:
time: 85.3 us; the launch traced here: 84.6 us
  Pallas kernels  82.9 us (97%)
  local copies, waits for them, and re-layouts  1.72 us (2%)
    pallas_call x1, Pallas kernels, body(): pl.pallas_call(functools.partial(kernel, (n_row, n_col, n_req)), name='pu...  82.9 us
    reshape x1, local copies, waits for them, and re-layouts, body(): return out.reshape(bs // 2, sr, 1, n_out, bs)  1.72 us

profile of v3, /device:TPU:6, one launch (start us, length us, event | category | flops | bytes accessed | tf_op | source)
XLA Modules:
  0.0 84.6 jit_solution(403722074373786205)
XLA Ops:
  0.0 82.9 %purify.1 = bf16[256,512]{1,0:T(8,128)(2,1)} custom-call(bf16[8,2,128,128]{3,2,1,0:T(8,128)(2,1)} %bitcast.8, bf16[8,2,128,128]{3,2,1,0:T(8,128)(2,1)} %bitcast.9, bf16[4096,128]{1,0:T(8,128)(2,1)} %bitcast.7, s32[1,2,8]{2,1,0:T(2,128)} %bitcast.11, s32[1,2,8]{2,1,0:T(2,128)} %bitcast.12, s32[1,8,64]{2,1,0:T(8,128)} %bitcast.10, s32[1,1,4]{2,1,0:T(1,128)} %oc_hbm.1), custom_call_target="tpu_custom_call" | custom-call | tf_op jit(solution)/shard_map/purify/pallas_call | solution.py:381
  82.9 1.7 %reshape.15 = bf16[64,4,1,4,128]{4,3,1,0,2:T(4,128)(2,1)} reshape(bf16[256,512]{1,0:T(8,128)(2,1)} %purify.1) | data formatting | bytes 524288 | tf_op jit(solution)/shard_map/reshape | solution.py:424

commit v4 on v3

--- a/solution.py
+++ b/solution.py
@@ -14,7 +14,7 @@
 NCH = len(CHUNKS)
 GROUPS = (1,)
 PIECES = (
-    (0, 0, 16), (0, 16, 32), (0, 48, 64), (0, 112, 16), (-1, 0, 1), (1, 0, 128), (2, 0, 128), (3, 0, 128),
+    (0, 0, 32), (0, 32, 64), (0, 96, 32), (-1, 0, 1), (1, 0, 128), (2, 0, 128), (3, 0, 128),
 )
 
 
@@ -26,8 +26,8 @@
     return lax.broadcasted_iota(jnp.int32, shape, dim)
 
 
-IDS = 4
-GATED = 6
+IDS = 3
+GATED = 5
 
 
 def piece(p, count):
@@ -215,12 +215,10 @@
         reader = lax.rem(row - stride * q + n_row, n_row)
         owners.append(lax.rem(req[0, q, reader], n_col))
 
-    build(3)
-    send(3)
     build_ids()
     send(IDS)
-    build(5)
-    send(5)
+    build(4)
+    send(4)
 
     group = BS // n_req
     to_row, from_row = iota((BS, BS), 0), iota((BS, BS), 1)
@@ -247,14 +245,12 @@
     upper((0, 1, 2), middle, True)
     forward(3)
     upper((3,), (*near, *middle), False)
-    build(6)
-    send(6)
+    build(5)
+    send(5)
     forward(4)
     upper((4,), (*near, *middle), False)
-    forward(5)
-    upper((5,), (*near, *middle), False)
     upper(range(GATED), far, True)
-    for p in range(7, n_p):
+    for p in range(6, n_p):
         build(p)
         send(p)
     loads[2].wait()

time: 85.3 us -> 84.9 us (level)
  no operation moved by 1% of the time
where the time goes in v4:
time: 84.9 us; the launch traced here: 84.3 us
  Pallas kernels  82.6 us (97%)
  local copies, waits for them, and re-layouts  1.72 us (2%)
    pallas_call x1, Pallas kernels, body(): pl.pallas_call(functools.partial(kernel, (n_row, n_col, n_req)), name='pu...  82.6 us
    reshape x1, local copies, waits for them, and re-layouts, body(): return out.reshape(bs // 2, sr, 1, n_out, bs)  1.72 us

profile of v4, /device:TPU:6, one launch (start us, length us, event | category | flops | bytes accessed | tf_op | source)
XLA Modules:
  0.0 84.3 jit_solution(18430088547650372610)
XLA Ops:
  0.0 82.6 %purify.1 = bf16[256,512]{1,0:T(8,128)(2,1)} custom-call(bf16[8,2,128,128]{3,2,1,0:T(8,128)(2,1)} %bitcast.8, bf16[8,2,128,128]{3,2,1,0:T(8,128)(2,1)} %bitcast.9, bf16[4096,128]{1,0:T(8,128)(2,1)} %bitcast.7, s32[1,2,8]{2,1,0:T(2,128)} %bitcast.11, s32[1,2,8]{2,1,0:T(2,128)} %bitcast.12, s32[1,8,64]{2,1,0:T(8,128)} %bitcast.10, s32[1,1,4]{2,1,0:T(1,128)} %oc_hbm.1), custom_call_target="tpu_custom_call" | custom-call | tf_op jit(solution)/shard_map/purify/pallas_call | solution.py:377
  82.6 1.7 %reshape.15 = bf16[64,4,1,4,128]{4,3,1,0,2:T(4,128)(2,1)} reshape(bf16[256,512]{1,0:T(8,128)(2,1)} %purify.1) | data formatting | bytes 524288 | tf_op jit(solution)/shard_map/reshape | solution.py:420
